TPU v7x, 32 devices: a whole 2x2x4 slice. The times are simulated.
32 devices in a mesh: depth: 4 (over y, x), surf: 8 (over z, core).
Axes of the slice: x: 2, y: 2, z: 4, core: 2. Of those that a mesh axis runs over, the one named last changes fastest.
Arguments:
- initial_warmth: float32 [256, 32, 2048], P('depth', 'surf'), may hold values from -6 to 6
- substance_label: int32 [256], replicated, may hold values from 0 to 3, never falling along the last dimension, each value on 1 to 128 neighbouring positions
- neighbour_kernel: float32 [4, 24], replicated, may hold values from 0.004 to 0.04
- arriving_heat_rate: float32 [32, 2048], P('surf'), may hold values from -3 to 3
- implicit_inverse_operator: float32 [256, 256], replicated, may hold values from 0 to 0.61, as said below
Outputs:
- final_temperature: float32 [256, 32, 2048], P('depth', 'surf')
Inputs may be any that keep to these rules, and one draw needn't show every extreme that they name: `substance_label`: material numbers never fall from layer 0 (the heated side) to the last layer; every material holds at least one layer. `implicit_inverse_operator`: all entries are positive.
All inputs are finite; a program needn't handle non-finite values.
Results may differ from a plain program's by a relative error of at most 0.0001.
Values sent between devices are 32-bit elements; how exact they have to be, the bound alone decides.
A program may use at most 64 MiB of HBM per device.

v0:
```python
import functools

import jax
import jax.numpy as jnp
from jax import lax
from jax.experimental import pallas as pl
from jax.experimental.pallas import tpu as pltpu
from jax.sharding import PartitionSpec as P

LANES = 128
REACH = 6
MESH = pl.DeviceIdType.MESH


def flipped(rank, mask, count):
    out, bit = 0, 1
    while bit < count:
        mine = (rank // bit) % 2
        out = out + bit * ((1 - mine) if (mask // bit) % 2 else mine)
        bit *= 2
    return out


def kernel(
    nd, ns, tiles,
    x_ref, lab_ref, nk_ref, heat_ref, op_ref, out_ref,
    raw, eraw, eb, hb, s0, s1, s2, ex, ob, coef, op3, lab,
    a_send, a_recv, a_loc, z_send, z_recv,
    h_send, h_recv, x_send, x_recv, o_send, o_recv, o_loc,
):
    d = lax.axis_index("depth")
    s = lax.axis_index("surf")
    layers_here = x_ref.shape[0]
    layers = op_ref.shape[0]
    width = heat_ref.shape[1]
    cols = tiles * LANES
    ring = tiles + 1
    peers = [j for j in range(nd - 1, 0, -1)]
    has = (s > 0, s < ns - 1)
    near = (s - 1, s + 1)
    mine = pl.ds(pl.multiple_of(d * layers_here, 8), layers_here)

    barrier = pltpu.get_barrier_semaphore()
    for j in peers:
        pl.semaphore_signal(
            barrier, inc=1, device_id={"depth": flipped(d, j, nd)}, device_id_type=MESH
        )
    for side in range(2):
        @pl.when(has[side])
        def _():
            pl.semaphore_signal(
                barrier, inc=1, device_id={"surf": near[side]}, device_id_type=MESH
            )
    at_end = jnp.where(s > 0, 0, 1) + jnp.where(s < ns - 1, 0, 1)
    pl.semaphore_wait(barrier, nd + 1 - at_end)

    def block_cols(b, t):
        return pl.ds(pl.multiple_of(b * cols + t * LANES, LANES), LANES)

    def spread(j, t):
        p = flipped(d, j, nd)
        if t == tiles:
            src, dst = eb.at[p], eraw.at[1, mine]
        else:
            src, dst = x_ref.at[:, :, block_cols(p, t)], raw.at[1, t, mine]
        return pltpu.make_async_remote_copy(
            src, dst, a_send.at[j, t], a_recv.at[j, t],
            device_id={"depth": p}, device_id_type=MESH,
        )

    def keep(t):
        if t == tiles:
            return pltpu.make_async_copy(eb.at[d], eraw.at[1, mine], a_loc.at[t])
        return pltpu.make_async_copy(
            x_ref.at[:, :, block_cols(d, t)], raw.at[1, t, mine], a_loc.at[t]
        )

    def forward(side, j, t):
        p = flipped(d, j, nd)
        part = pl.ds(pl.multiple_of(p * layers_here, 8), layers_here)
        if t == tiles:
            src, dst = eb.at[d] if j == 0 else eraw.at[1, part], eraw.at[2 - 2 * side, part]
        else:
            src = x_ref.at[:, :, block_cols(d, t)] if j == 0 else raw.at[1, t, part]
            dst = raw.at[2 - 2 * side, t, part]
        return pltpu.make_async_remote_copy(
            src, dst, z_send.at[side, j, t], z_recv.at[side, j, t],
            device_id={"surf": near[side]}, device_id_type=MESH,
        )

    def forward_both(j, t):
        for side in range(2):
            @pl.when(has[side])
            def _():
                forward(side, j, t).start()

    def heat_out(side):
        return pltpu.make_async_remote_copy(
            heat_ref, hb.at[1 - side], h_send.at[side], h_recv.at[side],
            device_id={"surf": near[side]}, device_id_type=MESH,
        )

    def trade(side, t):
        return pltpu.make_async_remote_copy(
            s2.at[t, pl.ds(2 + 2 * side, 2)], s2.at[t, pl.ds(6 - 6 * side, 2)],
            x_send.at[side, t], x_recv.at[side, t],
            device_id={"surf": near[side]}, device_id_type=MESH,
        )

    def give_back(j, t):
        p = flipped(d, j, nd)
        theirs = pl.ds(pl.multiple_of(p * layers_here, 8), layers_here)
        return pltpu.make_async_remote_copy(
            ob.at[t, theirs], out_ref.at[:, :, block_cols(d, t)],
            o_send.at[j, t], o_recv.at[j, t],
            device_id={"depth": p}, device_id_type=MESH,
        )

    def put_home(t):
        return pltpu.make_async_copy(
            ob.at[t, mine], out_ref.at[:, :, block_cols(d, t)], o_loc.at[t]
        )

    for j in peers:
        spread(j, 0).start()
    forward_both(0, 0)
    lane8 = lax.broadcasted_iota(jnp.int32, (8, LANES), 1)
    for b in range(nd):
        @pl.loop(0, layers_here // 8)
        def _(g):
            rows = pl.ds(pl.multiple_of(g * 8, 8), 8)
            packed = jnp.zeros((8, LANES), jnp.float32)
            for r in range(4):
                edge = jnp.zeros((8, LANES), jnp.float32)
                if b < nd - 1:
                    ahead = x_ref[rows, r, (b + 1) * cols:(b + 1) * cols + LANES]
                    edge = jnp.where(lane8 < REACH, ahead, edge)
                if b > 0:
                    behind = x_ref[rows, r, b * cols - LANES:b * cols]
                    edge = jnp.where(lane8 >= LANES - REACH, behind, edge)
                packed = packed + (pltpu.roll(edge, 16 * r, 1) if r else edge)
            eb[b, rows, :] = packed
    for t in [tiles] + list(range(1, tiles)):
        for j in peers:
            spread(j, t).start()
        forward_both(0, t)
    for t in range(ring):
        keep(t).start()
    for side in range(2):
        @pl.when(has[side])
        def _():
            heat_out(side).start()

    for b in range(layers // LANES):
        row = lab_ref[:, b * LANES:(b + 1) * LANES].astype(jnp.float32)
        tall = jnp.transpose(jnp.broadcast_to(row, (LANES, LANES)))
        lab[b * LANES:(b + 1) * LANES, :] = tall

    @pl.loop(0, layers // 8)
    def _(g):
        rows = pl.ds(pl.multiple_of(g * 8, 8), 8)
        kind = lab[rows, :]
        is0, is1, is2 = kind < 0.5, kind < 1.5, kind < 2.5
        total = jnp.zeros((8, LANES), jnp.float32)
        for k in range(24):
            c = jnp.where(
                is0, nk_ref[0, k],
                jnp.where(is1, nk_ref[1, k], jnp.where(is2, nk_ref[2, k], nk_ref[3, k])),
            )
            coef[k if k < 12 else k + 1, rows, :] = c
            total = total + c
        coef[12, rows, :] = 1.0 - total

    high = op_ref[...].astype(jnp.bfloat16)
    op3[:, 0:layers] = high
    op3[:, layers:2 * layers] = high
    op3[:, 2 * layers:] = (op_ref[...] - high.astype(jnp.float32)).astype(jnp.bfloat16)

    for side in range(2):
        @pl.when(jnp.logical_not(has[side]))
        def _():
            for t in range(ring):
                for r in range(2):
                    s2[t, 6 * side + r, :, :] = jnp.zeros((layers, LANES), jnp.float32)
                for r in range(4):
                    s0[t, 8 * side + r, :, :] = jnp.zeros((layers, LANES), jnp.float32)
            hb[side, :, :] = jnp.zeros((4, width), jnp.float32)

    for side in range(2):
        @pl.when(has[side])
        def _():
            heat_out(side).wait_send()
            heat_out(1 - side).wait_recv()

    row_keep = [jnp.where(h, 1.0, 0.0).astype(jnp.float32) for h in has]
    lane1 = lax.broadcasted_iota(jnp.int32, (1, LANES), 1)
    edge_keep = jnp.where(
        lane1 < REACH, jnp.where(d < nd - 1, 1.0, 0.0),
        jnp.where(lane1 >= LANES - REACH, jnp.where(d > 0, 1.0, 0.0), 0.0),
    ).astype(jnp.float32)

    def heat_row(row, t):
        if row < 0:
            src, r = hb.at[0], row + 4
        elif row > 3:
            src, r = hb.at[1], row - 4
        else:
            src, r = heat_ref, row
        if t < tiles:
            return src[r:r + 1, block_cols(d, t)]
        ahead = src[r:r + 1, block_cols(lax.rem(d + 1, nd), 0)]
        behind = src[r:r + 1, block_cols(lax.rem(d + nd - 1, nd), tiles - 1)]
        return jnp.where(lane1 < REACH, ahead, behind)

    def lateral(src, t, made, first):
        left, right = (t - 1) % ring, (t + 1) % ring

        @pl.loop(0, layers // 8, unroll=4)
        def _(g):
            rows = pl.ds(pl.multiple_of(g * 8, 8), 8)
            acc = [None] * made
            for q in (2, 1, 3, 0, 4):
                cs = [coef[p * 5 + q, rows, :] for p in range(5)]
                for i in range(made + 4):
                    view = src[t, i, rows, :]
                    if q < 2:
                        view = jnp.where(lane8 >= LANES - 2 + q, src[left, i, rows, :], view)
                        view = pltpu.roll(view, 2 - q, 1)
                    elif q > 2:
                        view = jnp.where(lane8 < q - 2, src[right, i, rows, :], view)
                        view = pltpu.roll(view, LANES + 2 - q, 1)
                    for r in range(max(0, i - 4), min(made, i + 1)):
                        term = cs[i - r] * view
                        acc[r] = term if acc[r] is None else acc[r] + term
            for r in range(made):
                ex[rows, r * LANES:(r + 1) * LANES] = acc[r]

        top = lax.broadcasted_iota(jnp.int32, (8, LANES), 0) == 0
        for r in range(made):
            lanes = slice(r * LANES, (r + 1) * LANES)
            heat = jnp.broadcast_to(heat_row(first + r, t), (8, LANES))
            ex[0:8, lanes] = ex[0:8, lanes] + jnp.where(top, heat, 0.0)

    def implicit(t, made, first, store):
        for pair in range(made // 2):
            e = ex[:, pair * 2 * LANES:(pair + 1) * 2 * LANES]
            if first < 0 and pair == 0:
                e = e * row_keep[0]
            if first < 0 and pair == made // 2 - 1:
                e = e * row_keep[1]
            if t == tiles:
                e = e * jnp.concatenate([edge_keep, edge_keep], axis=1)
            eh = e.astype(jnp.bfloat16)
            el = (e - eh.astype(jnp.float32)).astype(jnp.bfloat16)
            y = jnp.dot(
                op3[...], jnp.concatenate([eh, el, eh], axis=0),
                preferred_element_type=jnp.float32,
            )
            store(2 * pair, y[:, :LANES])
            store(2 * pair + 1, y[:, LANES:])

    done = set()
    arrival = [0, tiles] + list(range(1, tiles))

    def once(f):
        def g(t):
            if (f.__name__, t) not in done:
                done.add((f.__name__, t))
                f(t)
        return g

    @once
    def arrive(t):
        at = arrival.index(t)
        if at:
            arrive(arrival[at - 1])
        for j in peers:
            spread(j, t).wait_recv()
            forward_both(j, t)
        keep(t).wait()

    @once
    def unpack(t):
        at = arrival.index(t)
        arrive(arrival[min(at + 1, tiles)])

        def relayout(part):
            if t == tiles:
                @pl.loop(0, layers // 8)
                def _(g):
                    rows = pl.ds(pl.multiple_of(g * 8, 8), 8)
                    packed = eraw[part, rows, :]
                    wanted = jnp.logical_or(lane8 < REACH, lane8 >= LANES - REACH)
                    for r in range(4):
                        v = pltpu.roll(packed, LANES - 16 * r, 1) if r else packed
                        s0[t, 4 * part + r, rows, :] = jnp.where(wanted, v, 0.0)
            else:
                @pl.loop(0, layers // 8)
                def _(g):
                    rows = pl.ds(pl.multiple_of(g * 8, 8), 8)
                    for r in range(4):
                        s0[t, 4 * part + r, rows, :] = raw[part, t, rows, r, :]

        relayout(1)
        for side in range(2):
            @pl.when(has[side])
            def _():
                for j in range(nd):
                    forward(1 - side, j, t).wait_recv()
                relayout(2 * side)

    @once
    def step1(t):
        for u in (t, (t - 1) % ring, (t + 1) % ring):
            unpack(u)
        lateral(s0, t, 8, -2)

        def store(r, y):
            s1[t, r, :, :] = y
        implicit(t, 8, -2, store)

    @once
    def step2(t):
        for u in ((t - 1) % ring, t, (t + 1) % ring):
            step1(u)
        lateral(s1, t, 4, 0)

        def store(r, y):
            s2[t, 2 + r, :, :] = y
        implicit(t, 4, 0, store)
        for side in range(2):
            @pl.when(has[side])
            def _():
                trade(side, t).start()

    @once
    def halo(t):
        for side in range(2):
            @pl.when(has[side])
            def _():
                trade(1 - side, t).wait_recv()

    @once
    def step3(t):
        around = (t, (t - 1) % ring, (t + 1) % ring)
        for u in around:
            step2(u)
        for u in around:
            halo(u)
        lateral(s2, t, 4, 0)

        def store(r, y):
            ob[t, :, r, :] = y
        implicit(t, 4, 0, store)
        for j in peers:
            give_back(j, t).start()
        put_home(t).start()

    order = list(range(1, tiles)) + [0]
    for t in order:
        step3(t)

    for t in order:
        for j in peers:
            give_back(j, t).wait()
        put_home(t).wait()
    for t in range(ring):
        for j in peers:
            spread(j, t).wait_send()
        for side in range(2):
            @pl.when(has[side])
            def _():
                for j in range(nd):
                    forward(side, j, t).wait_send()
                trade(side, t).wait_send()


def shards(
    nd, ns,
    initial_warmth, substance_label, neighbour_kernel, arriving_heat_rate, implicit_inverse_operator,
):
    layers_here, rows, width = initial_warmth.shape
    layers = implicit_inverse_operator.shape[0]
    tiles = width // nd // LANES
    ring = tiles + 1
    labels = substance_label[None, :]
    f32, dma = jnp.float32, pltpu.SemaphoreType.DMA
    vmem = pl.BlockSpec(memory_space=pltpu.VMEM)
    return pl.pallas_call(
        functools.partial(kernel, nd, ns, tiles),
        out_shape=jax.ShapeDtypeStruct(initial_warmth.shape, f32),
        in_specs=[vmem, vmem, pl.BlockSpec(memory_space=pltpu.SMEM), vmem, vmem],
        out_specs=pl.BlockSpec(memory_space=pl.ANY),
        scratch_shapes=[
            pltpu.VMEM((3, tiles, layers, rows, LANES), f32),
            pltpu.VMEM((3, layers, LANES), f32),
            pltpu.VMEM((nd, layers_here, LANES), f32),
            pltpu.VMEM((2, rows, width), f32),
            pltpu.VMEM((ring, 3 * rows, layers, LANES), f32),
            pltpu.VMEM((ring, 2 * rows, layers, LANES), f32),
            pltpu.VMEM((ring, 2 * rows, layers, LANES), f32),
            pltpu.VMEM((layers, 2 * rows * LANES), f32),
            pltpu.VMEM((tiles, layers, rows, LANES), f32),
            pltpu.VMEM((25, layers, LANES), f32),
            pltpu.VMEM((layers, 3 * layers), jnp.bfloat16),
            pltpu.VMEM((layers, LANES), f32),
            dma((nd, ring)), dma((nd, ring)), dma((ring,)),
            dma((2, nd, ring)), dma((2, nd, ring)),
            dma((2,)), dma((2,)), dma((2, ring)), dma((2, ring)),
            dma((nd, tiles)), dma((nd, tiles)), dma((tiles,)),
        ],
        compiler_params=pltpu.CompilerParams(
            collective_id=0, has_side_effects=True, vmem_limit_bytes=60 * 1024 * 1024
        ),
    )(initial_warmth, labels, neighbour_kernel, arriving_heat_rate, implicit_inverse_operator)


def solution(mesh):
    return jax.shard_map(
        functools.partial(shards, mesh.shape["depth"], mesh.shape["surf"]),
        mesh=mesh,
        in_specs=(P("depth", "surf", None), P(), P(), P("surf", None), P()),
        out_specs=P("depth", "surf", None),
        check_vma=False,
    )
```

profile of v0, /device:TPU:9, one launch (start us, length us, event | category | flops | bytes accessed | tf_op | source)
XLA Modules:
  0.0 98.2 jit_solution(12815248708519905329)
XLA Ops:
  0.0 95.0 %shard_map.55 = f32[64,4,2048]{2,1,0:T(4,128)} custom-call(f32[64,4,2048]{2,1,0:T(4,128)} %x_ref.1, s32[1,256]{1,0:T(1,128)} %bitcast.1, f32[4,24]{1,0:T(4,128)} %nk_ref.1, f32[4,2048]{1,0:T(4,128)} %heat_ref.1, f32[256,256]{1,0:T(8,128)} %op_ref.1), custom_call_target="tpu_custom_call" | custom-call | tf_op jit(solution)/shard_map/pallas_call | solution.py:389
  95.0 3.2 %copy.7 = f32[64,4,2048]{2,1,0:T(4,128)} copy(f32[64,4,2048]{2,1,0:T(4,128)} %shard_map.55) | data formatting | bytes 4194304
where the time goes:
time: 98.4 us; the launch traced here: 98.2 us
  Pallas kernels  95 us (97%)
  local copies, waits for them, and re-layouts  3.16 us (3%)
    pallas_call x1, Pallas kernels, shards(): pl.pallas_call(functools.partial(kernel, nd, ns, tiles), out_shape=jax.Sh...  95 us
    unnamed x1, local copies, waits for them, and re-layouts  3.16 us

commit v1 on v0

v1 whole, which is shorter than its diff:
```python
import functools

import jax
import jax.numpy as jnp
from jax import lax
from jax.experimental import pallas as pl
from jax.experimental.pallas import tpu as pltpu
from jax.sharding import PartitionSpec as P

LANES = 128
STRIP = 6
PAD = 16
SPAN = LANES + 2 * PAD
WIDE = LANES + 16
MESH = pl.DeviceIdType.MESH
NT = (((1,), (1,)), ((), ()))


def flipped(rank, mask, count):
    out, bit = 0, 1
    while bit < count:
        mine = (rank // bit) % 2
        out = out + bit * ((1 - mine) if (mask // bit) % 2 else mine)
        bit *= 2
    return out


def kernel(
    nd, ns, tiles,
    x_ref, lab_ref, nk_ref, heat_ref, op_ref, out_ref,
    xr, raw, eb, eraw, et, s0, s1, s2, hot, ex, ob, coef, op3, opt,
    l_sem, a_send, a_recv, a_loc, z_send, z_recv, o_send, o_recv, o_loc,
):
    d = lax.axis_index("depth")
    s = lax.axis_index("surf")
    layers_here, rows, width = x_ref.shape
    layers = op_ref.shape[0]
    halves = layers // LANES
    cols = tiles * LANES
    states = (s0, s1, s2)
    peers = [j for j in range(nd - 1, 0, -1)]
    has = (s > 0, s < ns - 1)
    near = (s - 1, s + 1)
    mine = pl.ds(pl.multiple_of(d * layers_here, 8), layers_here)

    def block_cols(b, t):
        return pl.ds(pl.multiple_of(b * cols + t * LANES, LANES), LANES)

    def load(r):
        return pltpu.make_async_copy(x_ref.at[:, r, :], xr.at[r], l_sem.at[r])

    def spread(j, t):
        p = flipped(d, j, nd)
        if t == tiles:
            src, dst = eb.at[p], eraw.at[mine]
        else:
            src, dst = xr.at[:, :, block_cols(p, t)], raw.at[t, :, mine]
        return pltpu.make_async_remote_copy(
            src, dst, a_send.at[j, t], a_recv.at[j, t],
            device_id={"depth": p}, device_id_type=MESH,
        )

    def keep(t):
        if t == tiles:
            src, dst = eb.at[d], eraw.at[mine]
        else:
            src, dst = xr.at[:, :, block_cols(d, t)], raw.at[t, :, mine]
        return pltpu.make_async_copy(src, dst, a_loc.at[t])

    def trade(n, t, side):
        part = pl.ds(PAD - STRIP + 2 * n, LANES + 2 * STRIP - 4 * n)
        return pltpu.make_async_remote_copy(
            states[n].at[t, :, pl.ds(2 + 2 * side, 2), part],
            states[n].at[t, :, pl.ds(6 - 6 * side, 2), part],
            z_send.at[n, t, side], z_recv.at[n, t, side],
            device_id={"surf": near[side]}, device_id_type=MESH,
        )

    def give_back(j, t, r):
        p = flipped(d, j, nd)
        theirs = pl.ds(pl.multiple_of(p * layers_here, 8), layers_here)
        return pltpu.make_async_remote_copy(
            ob.at[t, r, theirs], out_ref.at[:, r, block_cols(d, t)],
            o_send.at[j, t, r], o_recv.at[j, t, r],
            device_id={"depth": p}, device_id_type=MESH,
        )

    def put_home(t, r):
        return pltpu.make_async_copy(
            ob.at[t, r, mine], out_ref.at[:, r, block_cols(d, t)], o_loc.at[t, r]
        )

    for r in range(rows):
        load(r).start()

    barrier = pltpu.get_barrier_semaphore()
    for j in peers:
        pl.semaphore_signal(
            barrier, inc=1, device_id={"depth": flipped(d, j, nd)}, device_id_type=MESH
        )
    for side in range(2):
        @pl.when(has[side])
        def _():
            pl.semaphore_signal(
                barrier, inc=1, device_id={"surf": near[side]}, device_id_type=MESH
            )
    at_end = jnp.where(s > 0, 0, 1) + jnp.where(s < ns - 1, 0, 1)
    for r in range(rows):
        load(r).wait()
    pl.semaphore_wait(barrier, nd + 1 - at_end)

    for j in peers:
        spread(j, 0).start()

    lane8 = lax.broadcasted_iota(jnp.int32, (8, LANES), 1)
    group = LANES // rows
    for b in range(nd):
        @pl.loop(0, layers_here // 8)
        def _(g):
            part = pl.ds(pl.multiple_of(g * 8, 8), 8)
            packed = jnp.zeros((8, LANES), jnp.float32)
            for r in range(rows):
                edge = jnp.zeros((8, LANES), jnp.float32)
                for i in range(tiles):
                    at = b * cols + (i + 1) * LANES
                    if at < width:
                        v = xr[r, part, at:at + LANES]
                        v = jnp.where(lane8 < STRIP, v, 0.0)
                        shift = STRIP * i + group * r
                        edge = edge + (pltpu.roll(v, shift, 1) if shift else v)
                if b > 0:
                    v = xr[r, part, b * cols - LANES:b * cols]
                    v = jnp.where(lane8 >= LANES - STRIP, v, 0.0)
                    shift = (group * (r + 1)) % LANES
                    edge = edge + (pltpu.roll(v, shift, 1) if shift else v)
                packed = packed + edge
            eb[b, part, :] = packed
    for t in [tiles] + list(range(1, tiles)):
        for j in peers:
            spread(j, t).start()
    for t in range(tiles + 1):
        keep(t).start()

    for h in range(halves):
        kind = jnp.broadcast_to(lab_ref[:, h * LANES:(h + 1) * LANES], (8, LANES))
        total = jnp.zeros((8, LANES), jnp.float32)
        for k in range(24):
            c = jnp.where(
                kind == 0, nk_ref[0, k],
                jnp.where(kind == 1, nk_ref[1, k], jnp.where(kind == 2, nk_ref[2, k], nk_ref[3, k])),
            )
            coef[h, k if k < 12 else k + 1] = c
            total = total + c
        coef[h, 12] = 1.0 - total

    high = op_ref[...].astype(jnp.bfloat16)
    low = (op_ref[...] - high.astype(jnp.float32)).astype(jnp.bfloat16)
    op3[:, 0:layers] = high
    op3[:, layers:2 * layers] = high
    op3[:, 2 * layers:] = low
    turned = jnp.transpose(op_ref[...])
    high = turned.astype(jnp.bfloat16)
    low = (turned - high.astype(jnp.float32)).astype(jnp.bfloat16)
    opt[0:layers, :] = high
    opt[layers:2 * layers, :] = high
    opt[2 * layers:, :] = low

    top = lax.broadcasted_iota(jnp.int32, (LANES, LANES), 0) == 0
    for t in range(-1, tiles + 1):
        b = d if 0 <= t < tiles else (lax.rem(d + nd - 1, nd) if t < 0 else lax.rem(d + 1, nd))
        for r in range(rows):
            line = heat_ref[r:r + 1, block_cols(b, t % tiles)]
            tall = jnp.transpose(jnp.where(top, jnp.broadcast_to(line, (LANES, LANES)), 0.0))
            hot[r, (t + 1) * LANES:(t + 2) * LANES, :] = tall

    for side in range(2):
        @pl.when(jnp.logical_not(has[side]))
        def _():
            @pl.loop(0, tiles)
            def _(t):
                for state in states:
                    for h in range(halves):
                        for r in range(2):
                            state[t, h, 6 * side + r] = jnp.zeros((SPAN, LANES), jnp.float32)

    def lateral(src, t, first, groups):
        for h in range(halves):
            cs = [coef[h, k] for k in range(25)]

            @pl.loop(0, groups // 2)
            def _(g):
                at = pl.multiple_of(first + g * 16, 8)
                whole = [[], [], [], []]
                for u in range(2):
                    acc = [None] * rows
                    for i in range(rows + 4):
                        for q in range(5):
                            view = src[t, h, i, pl.ds(at + 8 * u + q - 2, 8), :]
                            for r in range(max(0, i - 4), min(rows, i + 1)):
                                term = cs[(i - r) * 5 + q] * view
                                acc[r] = term if acc[r] is None else acc[r] + term
                    for r in range(rows):
                        v = acc[r]
                        if h == 0:
                            v = v + hot[r, pl.ds(at + 8 * u + (t + 1) * LANES - PAD, 8), :]
                        whole[r].append(v)
                for r in range(rows):
                    v = jnp.concatenate(whole[r], axis=0)
                    eh = v.astype(jnp.bfloat16)
                    el = (v - eh.astype(jnp.float32)).astype(jnp.bfloat16)
                    here = pl.ds(pl.multiple_of(g * 16, 16), 16)
                    ex[r, here, h * LANES:(h + 1) * LANES] = eh
                    ex[r, here, layers + h * LANES:layers + (h + 1) * LANES] = el

    def implicit(t, dst):
        for r in range(rows):
            e = ex[r]
            y = jnp.dot(
                jnp.concatenate([e, e[:, :layers]], axis=1), opt[...],
                preferred_element_type=jnp.float32,
            )
            for h in range(halves):
                dst[t, h, 2 + r, PAD - 8:PAD - 8 + WIDE, :] = y[:, h * LANES:(h + 1) * LANES]
        if t == 0:
            @pl.when(d == 0)
            def _():
                for h in range(halves):
                    for r in range(rows):
                        dst[t, h, 2 + r, PAD - 8:PAD, :] = jnp.zeros((8, LANES), jnp.float32)
        if t == tiles - 1:
            @pl.when(d == nd - 1)
            def _():
                for h in range(halves):
                    for r in range(rows):
                        dst[t, h, 2 + r, PAD + LANES:PAD + LANES + 8, :] = jnp.zeros((8, LANES), jnp.float32)

    def trades(n, t):
        for side in range(2):
            @pl.when(has[side])
            def _():
                trade(n, t, side).start()

    def halo(n, t):
        for side in range(2):
            @pl.when(has[side])
            def _():
                trade(n, t, 1 - side).wait_recv()

    def arrive(t):
        if t == 0:
            for j in peers:
                spread(j, tiles).wait_recv()
            keep(tiles).wait()
            for h in range(halves):
                et[h] = jnp.transpose(eraw[h * LANES:(h + 1) * LANES, :])
        for j in peers:
            spread(j, t).wait_recv()
        keep(t).wait()
        for h in range(halves):
            for r in range(rows):
                s0[t, h, 2 + r, PAD:PAD + LANES, :] = jnp.transpose(
                    raw[t, r, h * LANES:(h + 1) * LANES, :]
                )
                if t == 0:
                    left = et[h, group * (r + 1) - 8:group * (r + 1), :]
                else:
                    left = s0[t - 1, h, 2 + r, PAD + LANES - 8:PAD + LANES, :]
                s0[t, h, 2 + r, PAD - 8:PAD, :] = left
                at = group * r + STRIP * t
                s0[t, h, 2 + r, PAD + LANES:PAD + LANES + 8, :] = et[h, at:at + 8, :]
        trades(0, t)

    def step(n, t):
        halo(n - 1, t)
        lateral(states[n - 1], t, PAD - 8, WIDE // 8)
        implicit(t, states[n])
        trades(n, t)

    def last(t):
        halo(2, t)
        lateral(s2, t, PAD, LANES // 8)
        for pair in range(rows // 2):
            e = jnp.concatenate([ex[2 * pair, 0:LANES], ex[2 * pair + 1, 0:LANES]], axis=0)
            y = lax.dot_general(
                op3[...], jnp.concatenate([e, e[:, :layers]], axis=1), NT,
                preferred_element_type=jnp.float32,
            )
            ob[t, 2 * pair] = y[:, :LANES]
            ob[t, 2 * pair + 1] = y[:, LANES:]
        for j in peers:
            for r in range(rows):
                give_back(j, t, r).start()
        for r in range(rows):
            put_home(t, r).start()

    for stage in range(tiles + 3):
        if stage < tiles:
            arrive(stage)
        if 0 <= stage - 1 < tiles:
            step(1, stage - 1)
        if 0 <= stage - 2 < tiles:
            step(2, stage - 2)
        if 0 <= stage - 3 < tiles:
            last(stage - 3)

    for t in range(tiles):
        for r in range(rows):
            for j in peers:
                give_back(j, t, r).wait()
            put_home(t, r).wait()
    for t in range(tiles + 1):
        for j in peers:
            spread(j, t).wait_send()
    for t in range(tiles):
        for n in range(3):
            for side in range(2):
                @pl.when(has[side])
                def _():
                    trade(n, t, side).wait_send()


def shards(
    nd, ns,
    initial_warmth, substance_label, neighbour_kernel, arriving_heat_rate, implicit_inverse_operator,
):
    layers_here, rows, width = initial_warmth.shape
    layers = implicit_inverse_operator.shape[0]
    tiles = width // nd // LANES
    halves = layers // LANES
    labels = substance_label[None, :]
    f32, dma = jnp.float32, pltpu.SemaphoreType.DMA
    vmem = pl.BlockSpec(memory_space=pltpu.VMEM)
    state = pltpu.VMEM((tiles, halves, rows + 4, SPAN, LANES), f32)
    return pl.pallas_call(
        functools.partial(kernel, nd, ns, tiles),
        out_shape=jax.ShapeDtypeStruct(initial_warmth.shape, f32),
        in_specs=[
            pl.BlockSpec(memory_space=pl.ANY), vmem, pl.BlockSpec(memory_space=pltpu.SMEM), vmem, vmem,
        ],
        out_specs=pl.BlockSpec(memory_space=pl.ANY),
        scratch_shapes=[
            pltpu.VMEM((rows, layers_here, width), f32),
            pltpu.VMEM((tiles, rows, layers, LANES), f32),
            pltpu.VMEM((nd, layers_here, LANES), f32),
            pltpu.VMEM((layers, LANES), f32),
            pltpu.VMEM((halves, LANES, LANES), f32),
            state, state, state,
            pltpu.VMEM((rows, (tiles + 2) * LANES, LANES), f32),
            pltpu.VMEM((rows, WIDE, 2 * layers), jnp.bfloat16),
            pltpu.VMEM((tiles, rows, layers, LANES), f32),
            pltpu.VMEM((halves, 25, 8, LANES), f32),
            pltpu.VMEM((layers, 3 * layers), jnp.bfloat16),
            pltpu.VMEM((3 * layers, layers), jnp.bfloat16),
            dma((rows,)),
            dma((nd, tiles + 1)), dma((nd, tiles + 1)), dma((tiles + 1,)),
            dma((3, tiles, 2)), dma((3, tiles, 2)),
            dma((nd, tiles, rows)), dma((nd, tiles, rows)), dma((tiles, rows)),
        ],
        compiler_params=pltpu.CompilerParams(
            collective_id=0, has_side_effects=True, vmem_limit_bytes=60 * 1024 * 1024
        ),
    )(initial_warmth, labels, neighbour_kernel, arriving_heat_rate, implicit_inverse_operator)


def solution(mesh):
    return jax.shard_map(
        functools.partial(shards, mesh.shape["depth"], mesh.shape["surf"]),
        mesh=mesh,
        in_specs=(P("depth", "surf", None), P(), P(), P("surf", None), P()),
        out_specs=P("depth", "surf", None),
        check_vma=False,
    )
```

time: 98.4 us -> 72.4 us (0.74)
  Pallas kernels: 95 us -> 69.1 us
    pallas_call x1, Pallas kernels: 95 us -> 69.1 us  [shards(): pl.pallas_call(functools.partial(kernel, nd, ns, tiles), out_shape=jax.Sh...]
where the time goes in v1:
time: 72.4 us; the launch traced here: 72.2 us
  Pallas kernels  69.1 us (95%)
  local copies, waits for them, and re-layouts  3.16 us (4%)
    pallas_call x1, Pallas kernels, shards(): pl.pallas_call(functools.partial(kernel, nd, ns, tiles), out_shape=jax.Sh...  69.1 us
    unnamed x1, local copies, waits for them, and re-layouts  3.16 us

profile of v1, /device:TPU:9, one launch (start us, length us, event | category | flops | bytes accessed | tf_op | source)
XLA Modules:
  0.0 72.2 jit_solution(12482916847094803374)
XLA Ops:
  0.0 69.1 %shard_map.55 = f32[64,4,2048]{2,1,0:T(4,128)} custom-call(f32[64,4,2048]{2,1,0:T(4,128)} %x_ref.1, s32[1,256]{1,0:T(1,128)} %bitcast.1, f32[4,24]{1,0:T(4,128)} %nk_ref.1, f32[4,2048]{1,0:T(4,128)} %heat_ref.1, f32[256,256]{1,0:T(8,128)} %op_ref.1), custom_call_target="tpu_custom_call" | custom-call | tf_op jit(solution)/shard_map/pallas_call | solution.py:334
  69.1 3.2 %copy.7 = f32[64,4,2048]{2,1,0:T(4,128)} copy(f32[64,4,2048]{2,1,0:T(4,128)} %shard_map.55) | data formatting | bytes 4194304

commit v2 on v1

v2 whole, which is shorter than its diff:
```python
import functools

import jax
import jax.numpy as jnp
from jax import lax
from jax.experimental import pallas as pl
from jax.experimental.pallas import tpu as pltpu
from jax.sharding import PartitionSpec as P

LANES = 128
STRIP = 6
PAD = 16
SPAN = LANES + 2 * PAD
WIDE = LANES + 16
MESH = pl.DeviceIdType.MESH
NT = (((1,), (1,)), ((), ()))


def flipped(rank, mask, count):
    out, bit = 0, 1
    while bit < count:
        mine = (rank // bit) % 2
        out = out + bit * ((1 - mine) if (mask // bit) % 2 else mine)
        bit *= 2
    return out


def kernel(
    nd, ns, tiles,
    x_ref, lab_hbm, nk_hbm, heat_hbm, op_hbm, out_ref,
    lab_ref, nk_ref, heat_ref, op_ref,
    xr, raw, side_raw, eb, eraw, et, side_et, hb, s0, s1, s2, hot, ex, ob, coef, op3, opt,
    i_sem, l_sem, a_send, a_recv, a_loc, f_send, f_recv, e_send, e_recv, h_send, h_recv,
    z_send, z_recv, o_send, o_recv, o_loc,
):
    d = lax.axis_index("depth")
    s = lax.axis_index("surf")
    layers_here, rows, width = x_ref.shape
    layers = op_ref.shape[0]
    halves = layers // LANES
    cols = tiles * LANES
    peers = [j for j in range(nd - 1, 0, -1)]
    has = (s > 0, s < ns - 1)
    near = (s - 1, s + 1)
    mine = pl.ds(pl.multiple_of(d * layers_here, 8), layers_here)

    def block_cols(b, t):
        return pl.ds(pl.multiple_of(b * cols + t * LANES, LANES), LANES)

    def fetch(k):
        src = (lab_hbm, nk_hbm, heat_hbm, op_hbm)[k]
        return pltpu.make_async_copy(src, (lab_ref, nk_ref, heat_ref, op_ref)[k], i_sem.at[k])

    def load(r):
        return pltpu.make_async_copy(x_ref.at[:, r, :], xr.at[r], l_sem.at[r])

    def spread(j, t):
        p = flipped(d, j, nd)
        if t == tiles:
            src, dst = eb.at[p], eraw.at[mine]
        else:
            src, dst = xr.at[:, :, block_cols(p, t)], raw.at[t, :, mine]
        return pltpu.make_async_remote_copy(
            src, dst, a_send.at[j, t], a_recv.at[j, t],
            device_id={"depth": p}, device_id_type=MESH,
        )

    def keep(t):
        if t == tiles:
            src, dst = eb.at[d], eraw.at[mine]
        else:
            src, dst = xr.at[:, :, block_cols(d, t)], raw.at[t, :, mine]
        return pltpu.make_async_copy(src, dst, a_loc.at[t])

    def forward(side, j, t):
        p = flipped(d, j, nd)
        part = pl.ds(pl.multiple_of(p * layers_here, 8), layers_here)
        src = raw.at[t, :, part] if j else xr.at[:, :, block_cols(d, t)]
        return pltpu.make_async_remote_copy(
            src, side_raw.at[t, 1 - side, :, part], f_send.at[side, j, t], f_recv.at[side, j, t],
            device_id={"surf": near[side]}, device_id_type=MESH,
        )

    def forward_strips(side):
        return pltpu.make_async_remote_copy(
            et, side_et.at[1 - side], e_send.at[side], e_recv.at[side],
            device_id={"surf": near[side]}, device_id_type=MESH,
        )

    def heat_out(side):
        return pltpu.make_async_remote_copy(
            heat_hbm, hb.at[1 - side], h_send.at[side], h_recv.at[side],
            device_id={"surf": near[side]}, device_id_type=MESH,
        )

    def trade(t, side, h):
        part = pl.ds(PAD - 2, LANES + 4)
        return pltpu.make_async_remote_copy(
            s2.at[t, h, pl.ds(2 + 2 * side, 2), part],
            s2.at[t, h, pl.ds(6 - 6 * side, 2), part],
            z_send.at[t, side, h], z_recv.at[t, side, h],
            device_id={"surf": near[side]}, device_id_type=MESH,
        )

    def at_sides(action):
        for side in range(2):
            @pl.when(has[side])
            def _():
                action(side)

    def give_back(j, t, r):
        p = flipped(d, j, nd)
        theirs = pl.ds(pl.multiple_of(p * layers_here, 8), layers_here)
        return pltpu.make_async_remote_copy(
            ob.at[t, r, theirs], out_ref.at[:, r, block_cols(d, t)],
            o_send.at[j, t, r], o_recv.at[j, t, r],
            device_id={"depth": p}, device_id_type=MESH,
        )

    def put_home(t, r):
        return pltpu.make_async_copy(
            ob.at[t, r, mine], out_ref.at[:, r, block_cols(d, t)], o_loc.at[t, r]
        )

    barrier = pltpu.get_barrier_semaphore()
    for j in peers:
        pl.semaphore_signal(
            barrier, inc=1, device_id={"depth": flipped(d, j, nd)}, device_id_type=MESH
        )
    for side in range(2):
        @pl.when(has[side])
        def _():
            pl.semaphore_signal(
                barrier, inc=1, device_id={"surf": near[side]}, device_id_type=MESH
            )
    at_end = jnp.where(s > 0, 0, 1) + jnp.where(s < ns - 1, 0, 1)
    for r in range(rows):
        load(r).start()
    for k in range(4):
        fetch(k).start()
    for r in range(rows):
        load(r).wait()
    pl.semaphore_wait(barrier, nd + 1 - at_end)

    own = 2
    spread(peers[0], 0).start()
    def first_sends(side):
        forward(side, 0, 0).start()
        heat_out(side).start()
        for t in range(1, min(own, tiles)):
            forward(side, 0, t).start()

    at_sides(first_sends)

    lane8 = lax.broadcasted_iota(jnp.int32, (8, LANES), 1)
    group = LANES // rows
    for b in range(nd):
        @pl.loop(0, layers_here // 8)
        def _(g):
            part = pl.ds(pl.multiple_of(g * 8, 8), 8)
            packed = jnp.zeros((8, LANES), jnp.float32)
            for r in range(rows):
                edge = jnp.zeros((8, LANES), jnp.float32)
                for i in range(tiles):
                    at = b * cols + (i + 1) * LANES
                    if at < width:
                        v = xr[r, part, at:at + LANES]
                        v = jnp.where(lane8 < STRIP, v, 0.0)
                        shift = STRIP * i + group * r
                        edge = edge + (pltpu.roll(v, shift, 1) if shift else v)
                if b > 0:
                    v = xr[r, part, b * cols - LANES:b * cols]
                    v = jnp.where(lane8 >= LANES - STRIP, v, 0.0)
                    shift = (group * (r + 1)) % LANES
                    edge = edge + (pltpu.roll(v, shift, 1) if shift else v)
                packed = packed + edge
            eb[b, part, :] = packed
    for j in peers:
        spread(j, tiles).start()
    for j in peers[1:]:
        spread(j, 0).start()
    for t in range(1, tiles):
        for j in peers:
            spread(j, t).start()
    for t in range(tiles + 1):
        keep(t).start()

    for k in range(4):
        fetch(k).wait()
    for h in range(halves):
        kind = jnp.broadcast_to(lab_ref[:, h * LANES:(h + 1) * LANES], (8, LANES))
        total = jnp.zeros((8, LANES), jnp.float32)
        for k in range(24):
            c = jnp.where(
                kind == 0, nk_ref[0, k],
                jnp.where(kind == 1, nk_ref[1, k], jnp.where(kind == 2, nk_ref[2, k], nk_ref[3, k])),
            )
            coef[h, k if k < 12 else k + 1] = c
            total = total + c
        coef[h, 12] = 1.0 - total

    high = op_ref[...].astype(jnp.bfloat16)
    low = (op_ref[...] - high.astype(jnp.float32)).astype(jnp.bfloat16)
    op3[:, 0:layers] = high
    op3[:, layers:2 * layers] = high
    op3[:, 2 * layers:] = low
    turned = jnp.transpose(op_ref[...])
    high = turned.astype(jnp.bfloat16)
    low = (turned - high.astype(jnp.float32)).astype(jnp.bfloat16)
    opt[0:layers, :] = high
    opt[layers:2 * layers, :] = high
    opt[2 * layers:, :] = low

    top = lax.broadcasted_iota(jnp.int32, (LANES, LANES), 0) == 0

    def heat_row(src, row, to):
        for t in range(-1, tiles + 1):
            b = d if 0 <= t < tiles else (lax.rem(d + nd - 1, nd) if t < 0 else lax.rem(d + 1, nd))
            line = src[row:row + 1, block_cols(b, t % tiles)]
            tall = jnp.transpose(jnp.where(top, jnp.broadcast_to(line, (LANES, LANES)), 0.0))
            hot[to, (t + 1) * LANES:(t + 2) * LANES, :] = tall

    for r in range(rows):
        heat_row(heat_ref, r, 2 + r)

    for side in range(2):
        @pl.when(jnp.logical_not(has[side]))
        def _():
            @pl.loop(0, tiles)
            def _(t):
                for h in range(halves):
                    for r in range(rows):
                        s0[t, h, 8 * side + r] = jnp.zeros((SPAN, LANES), jnp.float32)
                    for r in range(2):
                        s2[t, h, 6 * side + r] = jnp.zeros((SPAN, LANES), jnp.float32)

    def side_heat(side):
        heat_out(1 - side).wait_recv()
        for r in range(2):
            heat_row(hb.at[side], r + 2 - 2 * side, r + 6 * side)

    at_sides(side_heat)

    def lateral(src, t, first, groups, made, warm, ready=None):
        for h in range(halves):
            if ready is not None:
                ready(h)
            cs = [coef[h, k] for k in range(25)]

            @pl.loop(0, groups // 2)
            def _(g):
                at = pl.multiple_of(first + g * 16, 8)
                whole = [[] for _ in range(made)]
                for u in range(2):
                    acc = [None] * made
                    for i in range(made + 4):
                        for q in range(5):
                            view = src[t, h, i, pl.ds(at + 8 * u + q - 2, 8), :]
                            for r in range(max(0, i - 4), min(made, i + 1)):
                                term = cs[(i - r) * 5 + q] * view
                                acc[r] = term if acc[r] is None else acc[r] + term
                    for r in range(made):
                        v = acc[r]
                        if h == 0:
                            v = v + hot[warm + r, pl.ds(at + 8 * u + (t + 1) * LANES - PAD, 8), :]
                        whole[r].append(v)
                for r in range(made):
                    v = jnp.concatenate(whole[r], axis=0)
                    eh = v.astype(jnp.bfloat16)
                    el = (v - eh.astype(jnp.float32)).astype(jnp.bfloat16)
                    here = pl.ds(pl.multiple_of(g * 16, 16), 16)
                    ex[r, here, h * LANES:(h + 1) * LANES] = eh
                    ex[r, here, layers + h * LANES:layers + (h + 1) * LANES] = el

    def implicit(t, dst, made, to):
        for r in range(made):
            e = ex[r]
            y = jnp.dot(
                jnp.concatenate([e, e[:, :layers]], axis=1), opt[...],
                preferred_element_type=jnp.float32,
            )
            for h in range(halves):
                dst[t, h, to + r, PAD - 8:PAD - 8 + WIDE, :] = y[:, h * LANES:(h + 1) * LANES]
        for at, edge in ((PAD - 8, jnp.logical_and(t == 0, d == 0)),
                         (PAD + LANES, jnp.logical_and(t == tiles - 1, d == nd - 1))):
            if t not in (0, tiles - 1):
                continue

            @pl.when(edge)
            def _():
                for h in range(halves):
                    for r in range(made):
                        dst[t, h, to + r, at:at + 8, :] = jnp.zeros((8, LANES), jnp.float32)

    def receive(t, k):
        for j in (peers[k:k + 1] if k < 2 else peers[2:]):
            spread(j, t).wait_recv()
            at_sides(lambda side: forward(side, j, t).start())
        if t == 0 and k == 0:
            for j in peers:
                spread(j, tiles).wait_recv()
            keep(tiles).wait()
            for h in range(halves):
                et[h] = jnp.transpose(eraw[h * LANES:(h + 1) * LANES, :])
            at_sides(lambda side: forward_strips(side).start())
        if k == 2 and t + own < tiles:
            at_sides(lambda side: forward(side, 0, t + own).start())

    def unpack(t, src, strips, row, to):
        for h in range(halves):
            s0[t, h, to, PAD:PAD + LANES, :] = jnp.transpose(
                src[row, h * LANES:(h + 1) * LANES, :]
            )
            if t == 0:
                left = strips[h, group * (row + 1) - 8:group * (row + 1), :]
            else:
                left = s0[t - 1, h, to, PAD + LANES - 8:PAD + LANES, :]
            s0[t, h, to, PAD - 8:PAD, :] = left
            at = group * row + STRIP * t
            s0[t, h, to, PAD + LANES:PAD + LANES + 8, :] = strips[h, at:at + 8, :]

    def arrange(t):
        keep(t).wait()
        for r in range(rows):
            unpack(t, raw.at[t], et, r, rows + r)

    def arrange_side(t):
        def one(side):
            if t == 0:
                forward_strips(1 - side).wait_recv()
            for j in range(nd):
                forward(1 - side, j, t).wait_recv()
            for r in range(rows):
                unpack(t, side_raw.at[t, side], side_et.at[side], r, 2 * rows * side + r)

        at_sides(one)

    def step1(t):
        lateral(s0, t, PAD - 8, WIDE // 8, rows + 4, 0)
        implicit(t, s1, rows + 4, 0)
        for side in range(2):
            @pl.when(jnp.logical_not(has[side]))
            def _():
                for h in range(halves):
                    for r in range(2):
                        s1[t, h, 6 * side + r] = jnp.zeros((SPAN, LANES), jnp.float32)

    def step2(t):
        lateral(s1, t, PAD - 8, WIDE // 8, rows, 2)
        implicit(t, s2, rows, 2)
        for h in range(halves):
            at_sides(lambda side: trade(t, side, h).start())

    def last(t):
        def ready(h):
            at_sides(lambda side: trade(t, 1 - side, h).wait_recv())

        lateral(s2, t, PAD, LANES // 8, rows, 2, ready)
        for pair in range(rows // 2):
            e = jnp.concatenate([ex[2 * pair, 0:LANES], ex[2 * pair + 1, 0:LANES]], axis=0)
            y = lax.dot_general(
                op3[...], jnp.concatenate([e, e[:, :layers]], axis=1), NT,
                preferred_element_type=jnp.float32,
            )
            for r in range(2 * pair, 2 * pair + 2):
                ob[t, r] = y[:, (r % 2) * LANES:(r % 2 + 1) * LANES]
                for j in peers:
                    give_back(j, t, r).start()
                put_home(t, r).start()

    plan = (
        "P0", "Q0", "R0", "P1", "Q1", "a0", "h0", "R1", "10", "a1", "P2",
        "20", "h1", "11", "Q2", "R2", "21", "P3", "Q3", "30", "a2", "h2",
        "R3", "12", "31", "a3", "22", "h3", "13", "23", "32", "33",
    )
    for item in plan:
        t = int(item[1])
        if t < tiles:
            {
                "P": lambda: receive(t, 0), "Q": lambda: receive(t, 1), "R": lambda: receive(t, 2),
                "a": lambda: arrange(t), "h": lambda: arrange_side(t),
                "1": lambda: step1(t), "2": lambda: step2(t), "3": lambda: last(t),
            }[item[0]]()

    for t in range(tiles):
        for r in range(rows):
            for j in peers:
                give_back(j, t, r).wait()
            put_home(t, r).wait()
    for t in range(tiles + 1):
        for j in peers:
            spread(j, t).wait_send()
    def sent(side):
        forward_strips(side).wait_send()
        heat_out(side).wait_send()
        for t in range(tiles):
            for j in range(nd):
                forward(side, j, t).wait_send()
            for h in range(halves):
                trade(t, side, h).wait_send()

    at_sides(sent)


def shards(
    nd, ns,
    initial_warmth, substance_label, neighbour_kernel, arriving_heat_rate, implicit_inverse_operator,
):
    layers_here, rows, width = initial_warmth.shape
    layers = implicit_inverse_operator.shape[0]
    tiles = width // nd // LANES
    halves = layers // LANES
    labels = substance_label[None, :]
    f32, dma = jnp.float32, pltpu.SemaphoreType.DMA

    def state(high):
        return pltpu.VMEM((tiles, halves, high, SPAN, LANES), f32)

    return pl.pallas_call(
        functools.partial(kernel, nd, ns, tiles),
        out_shape=jax.ShapeDtypeStruct(initial_warmth.shape, f32),
        in_specs=[pl.BlockSpec(memory_space=pltpu.HBM)] * 5,
        out_specs=pl.BlockSpec(memory_space=pl.ANY),
        scratch_shapes=[
            pltpu.VMEM(labels.shape, labels.dtype),
            pltpu.SMEM(neighbour_kernel.shape, f32),
            pltpu.VMEM(arriving_heat_rate.shape, f32),
            pltpu.VMEM((layers, layers), f32),
            pltpu.VMEM((rows, layers_here, width), f32),
            pltpu.VMEM((tiles, rows, layers, LANES), f32),
            pltpu.VMEM((tiles, 2, rows, layers, LANES), f32),
            pltpu.VMEM((nd, layers_here, LANES), f32),
            pltpu.VMEM((layers, LANES), f32),
            pltpu.VMEM((halves, LANES, LANES), f32),
            pltpu.VMEM((2, halves, LANES, LANES), f32),
            pltpu.VMEM((2, rows, width), f32),
            state(rows + 8), state(rows + 4), state(rows + 4),
            pltpu.VMEM((rows + 4, (tiles + 2) * LANES, LANES), f32),
            pltpu.VMEM((rows + 4, WIDE, 2 * layers), jnp.bfloat16),
            pltpu.VMEM((tiles, rows, layers, LANES), f32),
            pltpu.VMEM((halves, 25, 8, LANES), f32),
            pltpu.VMEM((layers, 3 * layers), jnp.bfloat16),
            pltpu.VMEM((3 * layers, layers), jnp.bfloat16),
            dma((4,)), dma((rows,)),
            dma((nd, tiles + 1)), dma((nd, tiles + 1)), dma((tiles + 1,)),
            dma((2, nd, tiles)), dma((2, nd, tiles)), dma((2,)), dma((2,)), dma((2,)), dma((2,)),
            dma((tiles, 2, halves)), dma((tiles, 2, halves)),
            dma((nd, tiles, rows)), dma((nd, tiles, rows)), dma((tiles, rows)),
        ],
        compiler_params=pltpu.CompilerParams(
            collective_id=0, has_side_effects=True, vmem_limit_bytes=60 * 1024 * 1024
        ),
    )(initial_warmth, labels, neighbour_kernel, arriving_heat_rate, implicit_inverse_operator)


def solution(mesh):
    return jax.shard_map(
        functools.partial(shards, mesh.shape["depth"], mesh.shape["surf"]),
        mesh=mesh,
        in_specs=(P("depth", "surf", None), P(), P(), P("surf", None), P()),
        out_specs=P("depth", "surf", None),
        check_vma=False,
    )
```

time: 72.4 us -> 67.8 us (0.936)
  Pallas kernels: 69.1 us -> 64.5 us
    pallas_call x1, Pallas kernels: 69.1 us -> 64.5 us  [shards(): pl.pallas_call(functools.partial(kernel, nd, ns, tiles), out_shape=jax.Sh...]
where the time goes in v2:
time: 67.8 us; the launch traced here: 67.6 us
  Pallas kernels  64.5 us (95%)
  local copies, waits for them, and re-layouts  3.16 us (5%)
    pallas_call x1, Pallas kernels, shards(): pl.pallas_call(functools.partial(kernel, nd, ns, tiles), out_shape=jax.Sh...  64.5 us
    unnamed x1, local copies, waits for them, and re-layouts  3.16 us

profile of v2, /device:TPU:9, one launch (start us, length us, event | category | flops | bytes accessed | tf_op | source)
XLA Modules:
  0.0 67.6 jit_solution(18244691512878327959)
XLA Ops:
  0.0 64.5 %shard_map.55 = f32[64,4,2048]{2,1,0:T(4,128)} custom-call(f32[64,4,2048]{2,1,0:T(4,128)} %x_ref.1, s32[1,256]{1,0:T(1,128)} %bitcast.1, f32[4,24]{1,0:T(4,128)} %nk_hbm.1, f32[4,2048]{1,0:T(4,128)} %heat_hbm.1, f32[256,256]{1,0:T(8,128)} %op_hbm.1), custom_call_target="tpu_custom_call" | custom-call | tf_op jit(solution)/shard_map/pallas_call | solution.py:419
  64.5 3.2 %copy.7 = f32[64,4,2048]{2,1,0:T(4,128)} copy(f32[64,4,2048]{2,1,0:T(4,128)} %shard_map.55) | data formatting | bytes 4194304

commit v3 on v2

--- a/solution.py
+++ b/solution.py
@@ -12,8 +12,43 @@
 PAD = 16
 SPAN = LANES + 2 * PAD
 WIDE = LANES + 16
+ROUND = 5
 MESH = pl.DeviceIdType.MESH
 NT = (((1,), (1,)), ((), ()))
+
+
+def spread_rows(x):
+    x0, x1, x2, x3, x4, x5, x6, x7 = x
+    mid = 2.5 * x3
+    e1, o1 = x2 + x6 - 4.25 * x4, x1 + x5 - 4.25 * x3
+    e2, o2 = 0.25 * x2 - 1.25 * x4 + x6, 0.5 * x1 - mid + 2.0 * x5
+    e3, o3 = 4.0 * x2 - 5.0 * x4 + x6, 2.0 * x1 - mid + 0.5 * x5
+    return [
+        x0 - x6 + 5.25 * (x4 - x2), e1 + o1, e1 - o1, e2 + o2, e2 - o2, e3 + o3, e3 - o3,
+        x7 - x1 + 5.25 * (x3 - x5),
+    ]
+
+
+def spread_taps(c):
+    c0, c1, c2, c3, c4 = c
+    f1, f2, f3 = -2.0 / 9.0, 1.0 / 90.0, 32.0 / 45.0
+    e1, o1 = c0 + c2 + c4, c1 + c3
+    e2, o2 = c0 + 4.0 * c2 + 16.0 * c4, 2.0 * c1 + 8.0 * c3
+    e3, o3 = c0 + 0.25 * c2 + 0.0625 * c4, 0.5 * c1 + 0.125 * c3
+    return [
+        c0, f1 * (e1 + o1), f1 * (e1 - o1), f2 * (e2 + o2), f2 * (e2 - o2),
+        f3 * (e3 + o3), f3 * (e3 - o3), c4,
+    ]
+
+
+def gather_rows(m):
+    s1, d1 = m[1] + m[2], m[1] - m[2]
+    s2, d2 = m[3] + m[4], m[3] - m[4]
+    s3, d3 = m[5] + m[6], m[5] - m[6]
+    return [
+        m[0] + s1 + s2 + s3, d1 + 2.0 * d2 + 0.5 * d3, s1 + 4.0 * s2 + 0.25 * s3,
+        d1 + 8.0 * d2 + 0.125 * d3 + m[7],
+    ]
 
 
 def flipped(rank, mask, count):
@@ -29,7 +64,7 @@
     nd, ns, tiles,
     x_ref, lab_hbm, nk_hbm, heat_hbm, op_hbm, out_ref,
     lab_ref, nk_ref, heat_ref, op_ref,
-    xr, raw, side_raw, eb, eraw, et, side_et, hb, s0, s1, s2, hot, ex, ob, coef, op3, opt,
+    xr, raw, side_raw, eb, eraw, et, side_et, hb, s0, s1, s2, hot, wide, ex, ob, coef, op3, opt,
     i_sem, l_sem, a_send, a_recv, a_loc, f_send, f_recv, e_send, e_recv, h_send, h_recv,
     z_send, z_recv, o_send, o_recv, o_loc,
 ):
@@ -190,14 +225,18 @@
     for h in range(halves):
         kind = jnp.broadcast_to(lab_ref[:, h * LANES:(h + 1) * LANES], (8, LANES))
         total = jnp.zeros((8, LANES), jnp.float32)
+        taps = []
         for k in range(24):
             c = jnp.where(
                 kind == 0, nk_ref[0, k],
                 jnp.where(kind == 1, nk_ref[1, k], jnp.where(kind == 2, nk_ref[2, k], nk_ref[3, k])),
             )
-            coef[h, k if k < 12 else k + 1] = c
+            taps.append(c)
             total = total + c
-        coef[h, 12] = 1.0 - total
+        taps.insert(12, 1.0 - total)
+        for q in range(5):
+            for i, c in enumerate(spread_taps(taps[q::5])):
+                coef[h, i * 5 + q] = c
 
     high = op_ref[...].astype(jnp.bfloat16)
     low = (op_ref[...] - high.astype(jnp.float32)).astype(jnp.bfloat16)
@@ -242,35 +281,56 @@
     at_sides(side_heat)
 
     def lateral(src, t, first, groups, made, warm, ready=None):
+        sets = made // 4
         for h in range(halves):
             if ready is not None:
                 ready(h)
-            cs = [coef[h, k] for k in range(25)]
-
-            @pl.loop(0, groups // 2)
+
+            turns = (groups + 2) // ROUND
+
+            @pl.loop(0, turns)
             def _(g):
-                at = pl.multiple_of(first + g * 16, 8)
-                whole = [[] for _ in range(made)]
-                for u in range(2):
-                    acc = [None] * made
-                    for i in range(made + 4):
-                        for q in range(5):
-                            view = src[t, h, i, pl.ds(at + 8 * u + q - 2, 8), :]
-                            for r in range(max(0, i - 4), min(made, i + 1)):
-                                term = cs[(i - r) * 5 + q] * view
-                                acc[r] = term if acc[r] is None else acc[r] + term
-                    for r in range(made):
-                        v = acc[r]
-                        if h == 0:
-                            v = v + hot[warm + r, pl.ds(at + 8 * u + (t + 1) * LANES - PAD, 8), :]
-                        whole[r].append(v)
-                for r in range(made):
-                    v = jnp.concatenate(whole[r], axis=0)
-                    eh = v.astype(jnp.bfloat16)
-                    el = (v - eh.astype(jnp.float32)).astype(jnp.bfloat16)
-                    here = pl.ds(pl.multiple_of(g * 16, 16), 16)
-                    ex[r, here, h * LANES:(h + 1) * LANES] = eh
-                    ex[r, here, layers + h * LANES:layers + (h + 1) * LANES] = el
+                for u in range(ROUND):
+                    here = pl.ds(pl.multiple_of(first - 8 + (g * ROUND + u) * 8, 8), 8)
+                    for k in range(sets):
+                        v = spread_rows([src[t, h, 4 * k + i, here, :] for i in range(8)])
+                        for i in range(8):
+                            wide[k, i, here, :] = v[i]
+
+            for u in range(turns * ROUND, groups + 2):
+                here = pl.ds(first - 8 + u * 8, 8)
+                for k in range(sets):
+                    v = spread_rows([src[t, h, 4 * k + i, here, :] for i in range(8)])
+                    for i in range(8):
+                        wide[k, i, here, :] = v[i]
+
+            per = 3 if groups % 6 == 0 else 4
+
+            @pl.loop(0, groups // (2 * per))
+            def _(g):
+                for w in range(per):
+                    at = pl.multiple_of(first + (g * per + w) * 16, 8)
+                    parts = [[[] for _ in range(sets)] for _ in range(2)]
+                    for i in range(8):
+                        cs = [coef[h, i * 5 + q] for q in range(5)]
+                        for u in range(2):
+                            for k in range(sets):
+                                m = None
+                                for q in range(5):
+                                    term = cs[q] * wide[k, i, pl.ds(at + 8 * u + q - 2, 8), :]
+                                    m = term if m is None else m + term
+                                parts[u][k].append(m)
+                    here = pl.ds(pl.multiple_of((g * per + w) * 16, 16), 16)
+                    for k in range(sets):
+                        both = [gather_rows(parts[u][k]) for u in range(2)]
+                        for r in range(4 * k, 4 * k + 4):
+                            v = jnp.concatenate([both[0][r - 4 * k], both[1][r - 4 * k]], axis=0)
+                            if h == 0:
+                                v = v + hot[warm + r, pl.ds(at + (t + 1) * LANES - PAD, 16), :]
+                            eh = v.astype(jnp.bfloat16)
+                            el = (v - eh.astype(jnp.float32)).astype(jnp.bfloat16)
+                            ex[r, here, h * LANES:(h + 1) * LANES] = eh
+                            ex[r, here, layers + h * LANES:layers + (h + 1) * LANES] = el
 
     def implicit(t, dst, made, to):
         for r in range(made):
@@ -416,7 +476,7 @@
     def state(high):
         return pltpu.VMEM((tiles, halves, high, SPAN, LANES), f32)
 
-    return pl.pallas_call(
+    return settled(pl.pallas_call(
         functools.partial(kernel, nd, ns, tiles),
         out_shape=jax.ShapeDtypeStruct(initial_warmth.shape, f32),
         in_specs=[pl.BlockSpec(memory_space=pltpu.HBM)] * 5,
@@ -436,9 +496,10 @@
             pltpu.VMEM((2, rows, width), f32),
             state(rows + 8), state(rows + 4), state(rows + 4),
             pltpu.VMEM((rows + 4, (tiles + 2) * LANES, LANES), f32),
+            pltpu.VMEM(((rows + 4) // 4, 8, SPAN, LANES), f32),
             pltpu.VMEM((rows + 4, WIDE, 2 * layers), jnp.bfloat16),
             pltpu.VMEM((tiles, rows, layers, LANES), f32),
-            pltpu.VMEM((halves, 25, 8, LANES), f32),
+            pltpu.VMEM((halves, 40, 8, LANES), f32),
             pltpu.VMEM((layers, 3 * layers), jnp.bfloat16),
             pltpu.VMEM((3 * layers, layers), jnp.bfloat16),
             dma((4,)), dma((rows,)),
@@ -450,7 +511,42 @@
         compiler_params=pltpu.CompilerParams(
             collective_id=0, has_side_effects=True, vmem_limit_bytes=60 * 1024 * 1024
         ),
-    )(initial_warmth, labels, neighbour_kernel, arriving_heat_rate, implicit_inverse_operator)
+    )(initial_warmth, labels, neighbour_kernel, arriving_heat_rate, implicit_inverse_operator))
+
+
+def settle(src_ref, out_ref, buf, i_sem, o_sem):
+    pieces = i_sem.shape[0]
+    each = src_ref.shape[0] // pieces
+
+    def copy(k, out):
+        part = pl.ds(k * each, each)
+        if out:
+            return pltpu.make_async_copy(buf.at[part], out_ref.at[part], o_sem.at[k])
+        return pltpu.make_async_copy(src_ref.at[part], buf.at[part], i_sem.at[k])
+
+    for k in range(pieces):
+        copy(k, False).start()
+    for k in range(pieces):
+        copy(k, False).wait()
+        copy(k, True).start()
+    for k in range(pieces):
+        copy(k, True).wait()
+
+
+def settled(x):
+    pieces = 8
+    hbm = pl.BlockSpec(memory_space=pltpu.HBM)
+    return pl.pallas_call(
+        settle,
+        out_shape=jax.ShapeDtypeStruct(x.shape, x.dtype),
+        in_specs=[hbm],
+        out_specs=hbm,
+        scratch_shapes=[
+            pltpu.VMEM(x.shape, x.dtype),
+            pltpu.SemaphoreType.DMA((pieces,)), pltpu.SemaphoreType.DMA((pieces,)),
+        ],
+        compiler_params=pltpu.CompilerParams(vmem_limit_bytes=60 * 1024 * 1024),
+    )(x)
 
 
 def solution(mesh):

time: 67.8 us -> 65.8 us (0.971)
  local copies, waits for them, and re-layouts: 3.16 us -> 0 us
  Pallas kernels: 64.5 us -> 65.4 us
    unnamed x1 -> x0, local copies, waits for them, and re-layouts: 3.16 us -> none
    pallas_call x0 -> x1, Pallas kernels: none -> 2.39 us  [settled(): pl.pallas_call(settle, out_shape=jax.ShapeDtypeStruct(x.shape, x.dtype),...]
    pallas_call x1, Pallas kernels: 64.5 us -> 63.1 us  [shards(): pl.pallas_call(functools.partial(kernel, nd, ns, tiles), out_shape=jax.Sh...]
where the time goes in v3:
time: 65.8 us; the launch traced here: 65.6 us
  Pallas kernels  65.4 us (99%)
    pallas_call x1, Pallas kernels, shards(): pl.pallas_call(functools.partial(kernel, nd, ns, tiles), out_shape=jax.Sh...  63.1 us
    pallas_call x1, Pallas kernels, settled(): pl.pallas_call(settle, out_shape=jax.ShapeDtypeStruct(x.shape, x.dtype),...  2.39 us

profile of v3, /device:TPU:9, one launch (start us, length us, event | category | flops | bytes accessed | tf_op | source)
XLA Modules:
  0.0 65.6 jit_solution(17969254153886672687)
XLA Ops:
  0.0 63.1 %shard_map.55.src_ref = f32[64,4,2048]{2,1,0:T(4,128)} custom-call(f32[64,4,2048]{2,1,0:T(4,128)} %x_ref.1, s32[1,256]{1,0:T(1,128)} %bitcast.1, f32[4,24]{1,0:T(4,128)} %nk_hbm.1, f32[4,2048]{1,0:T(4,128)} %heat_hbm.1, f32[256,256]{1,0:T(8,128)} %op_hbm.1), custom_call_target="tpu_custom_call" | custom-call | tf_op jit(solution)/shard_map/pallas_call | solution.py:479
  63.1 2.4 %shard_map.56 = f32[64,4,2048]{2,1,0:T(4,128)} custom-call(f32[64,4,2048]{2,1,0:T(4,128)} %shard_map.55.src_ref), custom_call_target="tpu_custom_call" | custom-call | tf_op jit(solution)/shard_map/pallas_call | solution.py:539

commit v4 on v3

--- a/solution.py
+++ b/solution.py
@@ -286,30 +286,29 @@
             if ready is not None:
                 ready(h)
 
-            turns = (groups + 2) // ROUND
+            def widen(u):
+                for k in range(sets):
+                    there = pl.ds(first - 2 + u * 8, 8)
+                    v = spread_rows([src[t, h, 4 * k + i, there, :] for i in range(8)])
+                    for i in range(8):
+                        wide[k, i, pl.ds(pl.multiple_of(u * 8, 8), 8), :] = v[i]
+
+            turns = (groups + 1) // ROUND
 
             @pl.loop(0, turns)
             def _(g):
                 for u in range(ROUND):
-                    here = pl.ds(pl.multiple_of(first - 8 + (g * ROUND + u) * 8, 8), 8)
-                    for k in range(sets):
-                        v = spread_rows([src[t, h, 4 * k + i, here, :] for i in range(8)])
-                        for i in range(8):
-                            wide[k, i, here, :] = v[i]
-
-            for u in range(turns * ROUND, groups + 2):
-                here = pl.ds(first - 8 + u * 8, 8)
-                for k in range(sets):
-                    v = spread_rows([src[t, h, 4 * k + i, here, :] for i in range(8)])
-                    for i in range(8):
-                        wide[k, i, here, :] = v[i]
+                    widen(g * ROUND + u)
+
+            for u in range(turns * ROUND, groups + 1):
+                widen(u)
 
             per = 3 if groups % 6 == 0 else 4
 
             @pl.loop(0, groups // (2 * per))
             def _(g):
                 for w in range(per):
-                    at = pl.multiple_of(first + (g * per + w) * 16, 8)
+                    at = pl.multiple_of((g * per + w) * 16, 16)
                     parts = [[[] for _ in range(sets)] for _ in range(2)]
                     for i in range(8):
                         cs = [coef[h, i * 5 + q] for q in range(5)]
@@ -317,7 +316,7 @@
                             for k in range(sets):
                                 m = None
                                 for q in range(5):
-                                    term = cs[q] * wide[k, i, pl.ds(at + 8 * u + q - 2, 8), :]
+                                    term = cs[q] * wide[k, i, pl.ds(at + 8 * u + q, 8), :]
                                     m = term if m is None else m + term
                                 parts[u][k].append(m)
                     here = pl.ds(pl.multiple_of((g * per + w) * 16, 16), 16)
@@ -326,21 +325,24 @@
                         for r in range(4 * k, 4 * k + 4):
                             v = jnp.concatenate([both[0][r - 4 * k], both[1][r - 4 * k]], axis=0)
                             if h == 0:
-                                v = v + hot[warm + r, pl.ds(at + (t + 1) * LANES - PAD, 16), :]
+                                v = v + hot[warm + r, pl.ds(at + first + (t + 1) * LANES - PAD, 16), :]
                             eh = v.astype(jnp.bfloat16)
                             el = (v - eh.astype(jnp.float32)).astype(jnp.bfloat16)
                             ex[r, here, h * LANES:(h + 1) * LANES] = eh
                             ex[r, here, layers + h * LANES:layers + (h + 1) * LANES] = el
 
-    def implicit(t, dst, made, to):
+    def implicit(t, dst, made, to, first, count):
         for r in range(made):
-            e = ex[r]
+            e = ex[r, 0:count]
             y = jnp.dot(
                 jnp.concatenate([e, e[:, :layers]], axis=1), opt[...],
                 preferred_element_type=jnp.float32,
             )
             for h in range(halves):
-                dst[t, h, to + r, PAD - 8:PAD - 8 + WIDE, :] = y[:, h * LANES:(h + 1) * LANES]
+                dst[t, h, to + r, first:first + count, :] = y[:, h * LANES:(h + 1) * LANES]
+                if t:
+                    old = dst[t - 1, h, to + r, first + LANES - 8:first + LANES, :]
+                    dst[t, h, to + r, first - 8:first, :] = old
         for at, edge in ((PAD - 8, jnp.logical_and(t == 0, d == 0)),
                          (PAD + LANES, jnp.logical_and(t == tiles - 1, d == nd - 1))):
             if t not in (0, tiles - 1):
@@ -395,9 +397,14 @@
 
         at_sides(one)
 
+    def advance(src, t, made, warm, dst, to, reach):
+        count = LANES if t else WIDE
+        first = PAD + LANES + reach - count
+        lateral(src, t, first, count // 8, made, warm)
+        implicit(t, dst, made, to, first, count)
+
     def step1(t):
-        lateral(s0, t, PAD - 8, WIDE // 8, rows + 4, 0)
-        implicit(t, s1, rows + 4, 0)
+        advance(s0, t, rows + 4, 0, s1, 0, 4)
         for side in range(2):
             @pl.when(jnp.logical_not(has[side]))
             def _():
@@ -406,8 +413,7 @@
                         s1[t, h, 6 * side + r] = jnp.zeros((SPAN, LANES), jnp.float32)
 
     def step2(t):
-        lateral(s1, t, PAD - 8, WIDE // 8, rows, 2)
-        implicit(t, s2, rows, 2)
+        advance(s1, t, rows, 2, s2, 2, 2)
         for h in range(halves):
             at_sides(lambda side: trade(t, side, h).start())
 

time: 65.8 us -> 64.9 us (0.986)
  Pallas kernels: 65.4 us -> 64.5 us
    pallas_call x1, Pallas kernels: 63.1 us -> 62.1 us  [shards(): pl.pallas_call(functools.partial(kernel, nd, ns, tiles), out_shape=jax.Sh...]
where the time goes in v4:
time: 64.9 us; the launch traced here: 64.7 us
  Pallas kernels  64.5 us (99%)
    pallas_call x1, Pallas kernels, shards(): pl.pallas_call(functools.partial(kernel, nd, ns, tiles), out_shape=jax.Sh...  62.1 us
    pallas_call x1, Pallas kernels, settled(): pl.pallas_call(settle, out_shape=jax.ShapeDtypeStruct(x.shape, x.dtype),...  2.39 us

profile of v4, /device:TPU:9, one launch (start us, length us, event | category | flops | bytes accessed | tf_op | source)
XLA Modules:
  0.0 64.7 jit_solution(5058453809336358741)
XLA Ops:
  0.0 62.1 %shard_map.55.src_ref = f32[64,4,2048]{2,1,0:T(4,128)} custom-call(f32[64,4,2048]{2,1,0:T(4,128)} %x_ref.1, s32[1,256]{1,0:T(1,128)} %bitcast.1, f32[4,24]{1,0:T(4,128)} %nk_hbm.1, f32[4,2048]{1,0:T(4,128)} %heat_hbm.1, f32[256,256]{1,0:T(8,128)} %op_hbm.1), custom_call_target="tpu_custom_call" | custom-call | tf_op jit(solution)/shard_map/pallas_call | solution.py:485
  62.1 2.4 %shard_map.56 = f32[64,4,2048]{2,1,0:T(4,128)} custom-call(f32[64,4,2048]{2,1,0:T(4,128)} %shard_map.55.src_ref), custom_call_target="tpu_custom_call" | custom-call | tf_op jit(solution)/shard_map/pallas_call | solution.py:545
